TPU v7x, 128 devices: a whole 4x4x4 slice. The times are simulated.
128 devices in a mesh: row: 8 (over z, core), col: 16 (over y, x).
Axes of the slice: x: 4, y: 4, z: 4, core: 2. Of those that a mesh axis runs over, the one named last changes fastest.
Arguments:
- emb: bfloat16 [524288, 512], P(('row', 'col')), may hold values from -6 to 6
- tiles: bfloat16 [2048, 4, 256, 256], P(('row', 'col')), may hold values from -0.375 to 0.375
- msg_src: int32 [2048, 4], P(('row', 'col')), may hold values from 0 to 15
- msg_dst: int32 [2048, 4], P(('row', 'col')), may hold values from 0 to 16, as said below
- msg_count: int32 [2048, 4], P(('row', 'col')), may hold values from 1 to 256
- weight: bfloat16 [512, 512], replicated, may hold values from -0.25 to 0.25
- docs: bfloat16 [512, 512], P('row'), may hold values from -0.059814453 to 0.099609375
- doc_labels: int32 [512, 8], replicated, may hold values from 0 to 524287
Outputs:
- hidden: bfloat16 [524288, 512], P(('row', 'col'))
- grad_docs: float32 [512, 512], P('row')
- grad_weight: float32 [512, 512], replicated
Inputs may be any that keep to these rules, and one draw needn't show every extreme that they name: For each sending device and each column of its row, the used slots (msg_dst below 16) come first and 16 marks an unused slot. In every row of devices some column receives all 4 slots used from every sender of that row.
All inputs are finite; a program needn't handle non-finite values.
Results may differ from a plain program's by a relative error of at most 0.0052.
Values may be sent and summed in bfloat16 or wider, within the bound.
No kernel may reach another device: no remote copies, remote signals or barrier semaphores. Data moves between devices by JAX's collectives and lax.ppermute only.
A program may use at most 192 MiB of HBM per device.

v0:
```python
import jax
import jax.numpy as jnp
from jax import lax
from jax.sharding import PartitionSpec as P


def per_device(emb, tiles, msg_src, msg_dst, msg_count, weight, docs, doc_labels):
    n_col = lax.axis_size("col")
    n_row = lax.axis_size("row")
    label_dev, width = emb.shape
    blk = tiles.shape[-1]
    cap = tiles.shape[1]
    blk_dev = label_dev // blk
    labels_total = float(label_dev * n_row * n_col)
    pos_count = doc_labels.shape[1]
    own_blocks = emb.reshape(blk_dev, blk, width)
    picked = own_blocks[msg_src]
    messages = jnp.einsum(
        "pqij,pqjd->pqid", tiles, picked, preferred_element_type=jnp.float32
    ).astype(jnp.bfloat16)
    received, dst_seen, cnt_seen = (
        lax.all_to_all(messages, "col", split_axis=0, concat_axis=0, tiled=True),
        lax.all_to_all(
            msg_dst.astype(jnp.bfloat16), "col", split_axis=0, concat_axis=0, tiled=True
        ),
        lax.all_to_all(
            msg_count.astype(jnp.bfloat16), "col", split_axis=0, concat_axis=0, tiled=True
        ),
    )
    slots_all = n_col * cap
    block_ids = jnp.arange(blk_dev, dtype=jnp.float32)
    hot = (dst_seen.astype(jnp.float32).reshape(1, slots_all) == block_ids[:, None]).astype(
        jnp.float32
    )
    weighted = hot * cnt_seen.astype(jnp.float32).reshape(1, slots_all)
    total = jnp.dot(
        weighted.astype(jnp.bfloat16),
        received.reshape(slots_all, blk * width),
        preferred_element_type=jnp.float32,
    ).reshape(blk_dev, blk, width)
    total = total + float(blk) * own_blocks.astype(jnp.float32)
    denom = float(blk) + jnp.sum(weighted, axis=1)
    agg = (total / denom[:, None, None]).astype(jnp.bfloat16).reshape(label_dev, width)
    pre = jnp.dot(agg, weight, preferred_element_type=jnp.float32)
    hidden = jax.nn.silu(pre).astype(jnp.bfloat16)
    device = lax.axis_index("row") * n_col + lax.axis_index("col")
    label_ids = device * label_dev + jnp.arange(label_dev, dtype=jnp.int32)
    piece = lax.all_gather(docs, "row", axis=0, tiled=True)
    scores = jnp.einsum("nd,ld->nl", piece, hidden, preferred_element_type=jnp.float32)
    positive = doc_labels[:, 0:1] == label_ids[None, :]
    for which in range(1, pos_count):
        positive = positive | (doc_labels[:, which : which + 1] == label_ids[None, :])
    prob = jax.nn.sigmoid(scores)
    dscore = jnp.where(positive, (prob - 1.0) / float(pos_count), prob / labels_total).astype(
        jnp.bfloat16
    )
    rows_grad = jnp.dot(dscore, hidden, preferred_element_type=jnp.float32)
    dhid = jnp.einsum("nl,nd->ld", dscore, piece, preferred_element_type=jnp.float32)
    doc_grad = rows_grad
    dhid, doc_grad = (dhid, doc_grad)
    sig = jax.nn.sigmoid(pre)
    dpre = (dhid * sig * (1.0 + pre * (1.0 - sig))).astype(jnp.bfloat16)
    weight_part = jnp.einsum("la,lb->ab", agg, dpre, preferred_element_type=jnp.float32)
    grad_weight = lax.psum(weight_part, ("row", "col"))
    row_share = lax.psum_scatter(doc_grad, "row", scatter_dimension=0, tiled=True)
    grad_docs = lax.psum(row_share, "col")
    return (hidden, grad_docs, grad_weight)


def solution(mesh):
    in_specs = (
        P(("row", "col"), None),
        P(("row", "col"), None, None, None),
        P(("row", "col"), None),
        P(("row", "col"), None),
        P(("row", "col"), None),
        P(),
        P("row", None),
        P(),
    )
    out_specs = (P(("row", "col"), None), P("row", None), P())
    return jax.shard_map(
        per_device, mesh=mesh, in_specs=in_specs, out_specs=out_specs, check_vma=False
    )
```

profile of v0, /device:TPU:0, one launch (start us, length us, event | category | flops | bytes accessed | tf_op | source)
XLA Modules:
  0.0 621.5 jit_solution(9641399624754386184)
XLA Ops:
  8.0 0.0 copy-start
  8.0 0.7 convert_bitcast_fusion.2
  8.8 0.7 copy.23
  9.5 7.1 %all-to-all-start = ((bf16[16,1,4]{2,1,0:T(2,128)(2,1)}), bf16[16,1,4]{2,1,0:T(2,128)(2,1)S(1)}, u32[]{:S(2)}, u32[]{:S(2)}) async-start(bf16[16,1,4]{2,1,0:T(2,128)(2,1)} %copy.23), calls=%async_computation | async-start | bytes 16384 | tf_op jit(solution)/shard_map/all_to_all | solution.py:23
  16.6 0.7 convert_bitcast_fusion.1
  17.3 0.7 copy.24
  18.0 0.7 compare_select_fusion
  18.7 0.1 copy.25
  18.8 0.1 reshape.51
  18.9 9.8 %gather_fusion = bf16[64,256,512]{2,1,0:T(8,128)(2,1)} fusion(bf16[16,256,512]{2,1,0:T(8,128)(2,1)} %bitcast.53, s32[1024]{0:T(1024)S(1)} %pad_clamp_fusion), kind=kCustom, calls=%fused_computation | custom fusion | bytes 33554688 | tf_op jit(solution)/shard_map/gather | solution.py:17
  28.6 0.0 all-to-all-done
  28.6 7.2 %all-to-all-start.1 = ((bf16[16,1,4]{2,1,0:T(2,128)(2,1)}), bf16[16,1,4]{2,1,0:T(2,128)(2,1)S(1)}, u32[]{:S(2)}, u32[]{:S(2)}) async-start(bf16[16,1,4]{2,1,0:T(2,128)(2,1)} %copy.24), calls=%async_computation.1 | async-start | bytes 16384 | tf_op jit(solution)/shard_map/all_to_all | solution.py:26
  35.9 19.3 %convert_bitcast_fusion = bf16[16,4,256,512]{2,3,1,0:T(8,128)(2,1)} fusion(bf16[16,4,256,512]{3,2,1,0:T(8,128)(2,1)} %bitcast.52, bf16[16,4,256,256]{3,2,1,0:T(8,128)(2,1)} %param.9), kind=kOutput, calls=%fused_computation.4 | convolution fusion | flops 4303355904 | bytes 41943040 | tf_op jit(solution)/shard_map/pqij,pqjd->pqid/dot_general | solution.py:18
  55.1 0.0 copy-start.6
  55.1 0.0 copy-start.5
  55.1 0.0 all-to-all-done.1
  55.1 7.4 %all-to-all-start.2 = ((bf16[16,4,256,512]{2,3,1,0:T(8,128)(2,1)}), bf16[16,4,256,512]{2,3,1,0:T(8,128)(2,1)}, u32[]{:S(2)}, u32[]{:S(2)}) async-start(bf16[16,4,256,512]{2,3,1,0:T(8,128)(2,1)} %convert_bitcast_fusion), calls=%async_computation.2 | async-start | bytes 33554432 | tf_op jit(solution)/shard_map/all_to_all | solution.py:22
  62.6 0.0 reduce-scatter.2.cloned.1.call-start
  62.6 0.0 copy-done.6
  62.7 0.0 copy-done.5
  62.7 14.5 %all_gather.3 = bf16[512,512]{1,0:T(8,128)(2,1)S(1)} all-gather(bf16[64,512]{1,0:T(8,128)(2,1)S(1)} %copy-done.5), channel_id=1, replica_groups=mesh['row'=8,'col'=16] {'row'}, dimensions={0}, use_global_device_ids=true | all-gather | bytes 589824 | tf_op jit(solution)/shard_map/all_gather | solution.py:48
  77.2 0.1 reshape.47
  77.3 0.1 reshape.48
  77.4 0.1 select_reduce_fusion
  77.5 229.1 %all-to-all-done.2 = bf16[16,4,256,512]{2,3,1,0:T(8,128)(2,1)} async-done(((bf16[16,4,256,512]{2,3,1,0:T(8,128)(2,1)}), bf16[16,4,256,512]{2,3,1,0:T(8,128)(2,1)}, u32[]{:S(2)}, u32[]{:S(2)}) %all-to-all-start.2) | async-done | bytes 16777248 | tf_op jit(solution)/shard_map/all_to_all | solution.py:22
  306.7 24.3 %copy.33 = bf16[8,8,256,512]{3,1,2,0:T(8,128)(2,1)} copy(bf16[8,8,256,512]{2,3,1,0:T(8,128)(2,1)} %bitcast.36) | data formatting | bytes 33554432
  331.0 9.2 %divide_convert_fusion = bf16[16,256,512]{2,0,1:T(8,128)(2,1)S(1)} fusion(bf16[16,256,512]{2,1,0:T(8,128)(2,1)} %bitcast.54, f32[16]{0:T(128)S(1)} %broadcast_add_fusion, f32[64]{0:T(128)S(1)} %reshape.48, f32[64]{0:T(128)S(1)} %reshape.47, bf16[8,8,256,512]{3,1,2,0:T(8,128)(2,1)} %copy.33), kind=kOutput, calls=%fused_computation.10 | convolution fusion | flops 278923264 | bytes 25166400 | tf_op jit(solution)/shard_map/dot_general | solution.py:36
  340.2 2.4 copy.30
  342.6 0.0 copy-start.4
  342.6 0.0 copy-done
  342.6 5.7 multiply_convert_fusion.1
  348.3 0.0 copy-done.4
  348.3 0.0 copy-start.2
  348.3 10.1 %fusion.3 = bf16[512,4096]{0,1:T(8,128)(2,1)S(1)} fusion(bf16[4096,512]{1,0:T(8,128)(2,1)S(1)} %get-tuple-element.13, bf16[512,512]{1,0:T(8,128)(2,1)S(1)} %all_gather.3, s32[512]{0:T(512)S(1)} %bitcast.63, s32[512]{0:T(512)S(1)} %bitcast.64, s32[512]{0:T(512)S(1)} %bitcast.58, s32[512]{0:T(512)S(1)} %bitcast.59, s32[512]{0:T(512)S(1)} %bitcast.60, ...), kind=kOutput, calls=%fused_computation.6 | convolution fusion | flops 2195718144 | bytes 8945664 | tf_op jit(solution)/shard_map/nd,ld->nl/dot_general | solution.py:49
  358.3 0.0 copy-done.2
  358.3 0.0 copy-start.3
  358.4 1.9 copy-done.3
  360.3 3.3 fusion.15
  363.6 0.0 reduce-scatter.2.cloned.1.call-update
  363.6 0.3 all-reduce.5.cloned.1.call-start
  363.9 0.0 copy-start.1
  363.9 12.6 %fusion.6 = f32[512,512]{1,0:T(8,128)} fusion(bf16[4096,512]{1,0:T(8,128)(2,1)} %bitcast.56, f32[4096,512]{1,0:T(8,128)} %get-tuple-element.12, bf16[512,4096]{0,1:T(8,128)(2,1)} %copy-done.3, bf16[512,512]{1,0:T(8,128)(2,1)S(1)} %all_gather.3), kind=kOutput, calls=%fused_computation.11 | convolution fusion | flops 4313841664 | bytes 18350080 | tf_op jit(solution)/shard_map/la,lb->ab/dot_general | solution.py:63
  376.5 0.0 all-reduce.5.cloned.1.call-update
  376.6 0.0 all-reduce.3.cloned.1.call-start
  376.6 21.8 %reduce-scatter.2.cloned.1.call-done = f32[64,512]{1,0:T(8,128)} async-done(((f32[512,512]{1,0:T(8,128)}), f32[64,512]{1,0:T(8,128)}) %reduce-scatter.2.cloned.1.call-update) | async-done | bytes 131088 | tf_op jit(solution)/shard_map/reduce_scatter | solution.py:65
  398.4 0.0 all-reduce.3.cloned.1.call-update
  398.5 127.3 %all-reduce.5.cloned.1.call-done = f32[512,512]{1,0:T(8,128)} async-done(((f32[512,512]{1,0:T(8,128)}), f32[512,512]{1,0:T(8,128)}) %all-reduce.5.cloned.1.call-update) | async-done | bytes 1048592 | tf_op jit(solution)/shard_map/psum | solution.py:64
  525.7 84.6 %all-reduce.3.cloned.1.call-done = f32[64,512]{1,0:T(8,128)} async-done(((f32[64,512]{1,0:T(8,128)}), f32[64,512]{1,0:T(8,128)}) %all-reduce.3.cloned.1.call-update) | async-done | bytes 131088 | tf_op jit(solution)/shard_map/psum | solution.py:66
  610.3 1.6 copy.44
  611.8 2.3 copy.45
  614.1 0.0 copy-done.1
  (6 shorter events, 0.1 us)
Async XLA Ops:
  8.0 334.6 %copy-start = (bf16[512,512]{1,0:T(8,128)(2,1)S(1)}, bf16[512,512]{1,0:T(8,128)(2,1)}, u32[]{:S(2)}) copy-start(bf16[512,512]{1,0:T(8,128)(2,1)} %param.13) | copy-start | bytes 1572868
  9.5 19.2 %all-to-all-start = ((bf16[16,1,4]{2,1,0:T(2,128)(2,1)}), bf16[16,1,4]{2,1,0:T(2,128)(2,1)S(1)}, u32[]{:S(2)}, u32[]{:S(2)}) async-start(bf16[16,1,4]{2,1,0:T(2,128)(2,1)} %copy.23), calls=%async_computation | async-start | bytes 16384 | tf_op jit(solution)/shard_map/all_to_all | solution.py:23
  28.6 26.5 %all-to-all-start.1 = ((bf16[16,1,4]{2,1,0:T(2,128)(2,1)}), bf16[16,1,4]{2,1,0:T(2,128)(2,1)S(1)}, u32[]{:S(2)}, u32[]{:S(2)}) async-start(bf16[16,1,4]{2,1,0:T(2,128)(2,1)} %copy.24), calls=%async_computation.1 | async-start | bytes 16384 | tf_op jit(solution)/shard_map/all_to_all | solution.py:26
  55.1 7.5 %copy-start.6 = (s32[512,8]{0,1:T(8,128)S(1)}, s32[512,8]{0,1:T(8,128)}, u32[]{:S(2)}) copy-start(s32[512,8]{0,1:T(8,128)} %param.15) | copy-start | bytes 49156
  55.1 7.5 %copy-start.5 = (bf16[64,512]{1,0:T(8,128)(2,1)S(1)}, bf16[64,512]{1,0:T(8,128)(2,1)}, u32[]{:S(2)}) copy-start(bf16[64,512]{1,0:T(8,128)(2,1)} %param.14) | copy-start | bytes 196612
  55.1 251.5 %all-to-all-start.2 = ((bf16[16,4,256,512]{2,3,1,0:T(8,128)(2,1)}), bf16[16,4,256,512]{2,3,1,0:T(8,128)(2,1)}, u32[]{:S(2)}, u32[]{:S(2)}) async-start(bf16[16,4,256,512]{2,3,1,0:T(8,128)(2,1)} %convert_bitcast_fusion), calls=%async_computation.2 | async-start | bytes 33554432 | tf_op jit(solution)/shard_map/all_to_all | solution.py:22
  62.6 335.9 %reduce-scatter.2.cloned.1.call-start = ((), (), s32[]{:S(2)}) async-start(), calls=%async_computation.4 | async-start | bytes 1179648 | tf_op jit(solution)/shard_map/reduce_scatter | solution.py:65
  342.6 5.7 copy-start.4
  348.3 10.1 %copy-start.2 = (bf16[4096,512]{1,0:T(8,128)(2,1)}, bf16[4096,512]{1,0:T(8,128)(2,1)S(1)}, u32[]{:S(2)}) copy-start(bf16[4096,512]{1,0:T(8,128)(2,1)S(1)} %get-tuple-element.13) | copy-start | bytes 12582916
  358.3 1.9 copy-start.3
  363.6 162.1 %all-reduce.5.cloned.1.call-start = ((), (), s32[]{:S(2)}) async-start(), calls=%async_computation.6 | async-start | bytes 2097152 | tf_op jit(solution)/shard_map/psum | solution.py:64
  363.9 250.2 %copy-start.1 = (bf16[512,512]{1,0:T(8,128)(2,1)S(1)}, bf16[512,512]{1,0:T(8,128)(2,1)}, u32[]{:S(2)}) copy-start(bf16[512,512]{1,0:T(8,128)(2,1)} %param.13) | copy-start | bytes 1572868
  376.6 233.7 %all-reduce.3.cloned.1.call-start = ((), (), s32[]{:S(2)}) async-start(), calls=%async_computation.5 | async-start | bytes 262144 | tf_op jit(solution)/shard_map/psum | solution.py:66
Sparse Core Ops, SparseCore 0:
  363.8 34.6 reduce-scatter.1
Sparse Core Ops, SparseCore 1:
  376.6 149.0 all-reduce.4
  528.8 81.4 all-reduce.2
where the time goes:
time: 623 us; the launch traced here: 622 us
  waiting for transfers between devices  463 us (74%)
  matrix products  60.1 us (10%)
  local copies, waits for them, and re-layouts  44 us (7%)
  starting transfers between devices  22.1 us (4%)
  between operations  15.7 us (3%)
  blocking collectives  14.5 us (2%)
    all_to_all x1, waiting for transfers between devices, per_device(): lax.all_to_all(messages, 'col', split_axis=0, concat_axis=0, tiled=True)  229 us
    psum x1, waiting for transfers between devices, per_device(): grad_weight = lax.psum(weight_part, ('row', 'col'))  127 us
    psum x1, waiting for transfers between devices, per_device(): grad_docs = lax.psum(row_share, 'col')  84.6 us
    unnamed x17, local copies, waits for them, and re-layouts  30.1 us
    reduce_scatter x1, waiting for transfers between devices, per_device(): lax.psum_scatter(doc_grad, 'row', scatter_dimension=0, tiled=True)  21.8 us
    dot_general x1, matrix products, per_device(): jnp.einsum('pqij,pqjd->pqid', tiles, picked, preferred_element_type=jnp.f...  19.3 us
    all_gather x1, blocking collectives, per_device(): piece = lax.all_gather(docs, 'row', axis=0, tiled=True)  14.5 us
    dot_general x1, matrix products, per_device(): jnp.einsum('la,lb->ab', agg, dpre, preferred_element_type=jnp.float32)  12.6 us
  transfers between devices with their start and end apart: 6, of which 4 were waited for; matrix products, arithmetic and copies ran while one was open for 7% of the time, Pallas kernels for 0%

commit v1 on v0

--- a/solution.py
+++ b/solution.py
@@ -2,6 +2,12 @@
 import jax.numpy as jnp
 from jax import lax
 from jax.sharding import PartitionSpec as P
+
+
+def clear_the_roots(mine_x, device_axis, mesh_ax):
+    for no in (device_axis, mesh_ax):
+        mine_x = jax.lax.psum(mine_x, no)
+    return mine_x
 
 
 def per_device(emb, tiles, msg_src, msg_dst, msg_count, weight, docs, doc_labels):
@@ -61,7 +67,7 @@
     sig = jax.nn.sigmoid(pre)
     dpre = (dhid * sig * (1.0 + pre * (1.0 - sig))).astype(jnp.bfloat16)
     weight_part = jnp.einsum("la,lb->ab", agg, dpre, preferred_element_type=jnp.float32)
-    grad_weight = lax.psum(weight_part, ("row", "col"))
+    grad_weight = clear_the_roots(weight_part, "col", mesh_ax="row")
     row_share = lax.psum_scatter(doc_grad, "row", scatter_dimension=0, tiled=True)
     grad_docs = lax.psum(row_share, "col")
     return (hidden, grad_docs, grad_weight)

time: 623 us -> 562 us (0.902)
  waiting for transfers between devices: 463 us -> 404 us
    psum x1, waiting for transfers between devices: 127 us -> 64.4 us  [clear_the_roots(): mine_x = jax.lax.psum(mine_x, no)]
  transfers between devices with their start and end apart: 6 -> 6, of which waited for: 4 -> 4; matrix products, arithmetic and copies ran while one was open for 7% -> 8% of each run, Pallas kernels for 0% -> 0%
where the time goes in v1:
time: 562 us; the launch traced here: 561 us
  waiting for transfers between devices  404 us (72%)
  matrix products  60.1 us (11%)
  local copies, waits for them, and re-layouts  44 us (8%)
  starting transfers between devices  22.1 us (4%)
  blocking collectives  14.5 us (3%)
  between operations  13.9 us (2%)
    all_to_all x1, waiting for transfers between devices, per_device(): lax.all_to_all(messages, 'col', split_axis=0, concat_axis=0, tiled=True)  229 us
    psum x1, waiting for transfers between devices, per_device(): grad_docs = lax.psum(row_share, 'col')  89 us
    psum x1, waiting for transfers between devices, clear_the_roots(): mine_x = jax.lax.psum(mine_x, no)  64.4 us
    unnamed x17, local copies, waits for them, and re-layouts  30.1 us
    reduce_scatter x1, waiting for transfers between devices, per_device(): lax.psum_scatter(doc_grad, 'row', scatter_dimension=0, tiled=True)  21.5 us
    dot_general x1, matrix products, per_device(): jnp.einsum('pqij,pqjd->pqid', tiles, picked, preferred_element_type=jnp.f...  19.3 us
    all_gather x1, blocking collectives, per_device(): piece = lax.all_gather(docs, 'row', axis=0, tiled=True)  14.5 us
    dot_general x1, matrix products, per_device(): jnp.einsum('la,lb->ab', agg, dpre, preferred_element_type=jnp.float32)  12.6 us
  transfers between devices with their start and end apart: 6, of which 4 were waited for; matrix products, arithmetic and copies ran while one was open for 8% of the time, Pallas kernels for 0%

profile of v1, /device:TPU:0, one launch (start us, length us, event | category | flops | bytes accessed | tf_op | source)
XLA Modules:
  0.0 561.1 jit_solution(8395262945396128657)
XLA Ops:
  7.2 0.0 copy-start
  7.2 0.7 convert_bitcast_fusion.2
  7.9 0.7 copy.23
  8.6 7.1 %all-to-all-start = ((bf16[16,1,4]{2,1,0:T(2,128)(2,1)}), bf16[16,1,4]{2,1,0:T(2,128)(2,1)S(1)}, u32[]{:S(2)}, u32[]{:S(2)}) async-start(bf16[16,1,4]{2,1,0:T(2,128)(2,1)} %copy.23), calls=%async_computation | async-start | bytes 16384 | tf_op jit(solution)/shard_map/all_to_all | solution.py:29
  15.8 0.7 convert_bitcast_fusion.1
  16.5 0.7 copy.24
  17.2 0.7 compare_select_fusion
  17.8 0.1 copy.25
  17.9 0.1 reshape.51
  18.0 9.8 %gather_fusion = bf16[64,256,512]{2,1,0:T(8,128)(2,1)} fusion(bf16[16,256,512]{2,1,0:T(8,128)(2,1)} %bitcast.53, s32[1024]{0:T(1024)S(1)} %pad_clamp_fusion), kind=kCustom, calls=%fused_computation | custom fusion | bytes 33554688 | tf_op jit(solution)/shard_map/gather | solution.py:23
  27.8 0.0 all-to-all-done
  27.8 7.2 %all-to-all-start.1 = ((bf16[16,1,4]{2,1,0:T(2,128)(2,1)}), bf16[16,1,4]{2,1,0:T(2,128)(2,1)S(1)}, u32[]{:S(2)}, u32[]{:S(2)}) async-start(bf16[16,1,4]{2,1,0:T(2,128)(2,1)} %copy.24), calls=%async_computation.1 | async-start | bytes 16384 | tf_op jit(solution)/shard_map/all_to_all | solution.py:32
  35.0 19.3 %convert_bitcast_fusion = bf16[16,4,256,512]{2,3,1,0:T(8,128)(2,1)} fusion(bf16[16,4,256,512]{3,2,1,0:T(8,128)(2,1)} %bitcast.52, bf16[16,4,256,256]{3,2,1,0:T(8,128)(2,1)} %param.9), kind=kOutput, calls=%fused_computation.4 | convolution fusion | flops 4303355904 | bytes 41943040 | tf_op jit(solution)/shard_map/pqij,pqjd->pqid/dot_general | solution.py:24
  54.3 0.0 copy-start.6
  54.3 0.0 copy-start.5
  54.3 0.0 all-to-all-done.1
  54.3 7.4 %all-to-all-start.2 = ((bf16[16,4,256,512]{2,3,1,0:T(8,128)(2,1)}), bf16[16,4,256,512]{2,3,1,0:T(8,128)(2,1)}, u32[]{:S(2)}, u32[]{:S(2)}) async-start(bf16[16,4,256,512]{2,3,1,0:T(8,128)(2,1)} %convert_bitcast_fusion), calls=%async_computation.2 | async-start | bytes 33554432 | tf_op jit(solution)/shard_map/all_to_all | solution.py:28
  61.7 0.0 reduce-scatter.2.cloned.1.call-start
  61.8 0.0 copy-done.6
  61.8 0.0 copy-done.5
  61.8 14.5 %all_gather.3 = bf16[512,512]{1,0:T(8,128)(2,1)S(1)} all-gather(bf16[64,512]{1,0:T(8,128)(2,1)S(1)} %copy-done.5), channel_id=1, replica_groups=mesh['row'=8,'col'=16] {'row'}, dimensions={0}, use_global_device_ids=true | all-gather | bytes 589824 | tf_op jit(solution)/shard_map/all_gather | solution.py:54
  76.3 0.1 reshape.47
  76.5 0.1 reshape.48
  76.5 0.1 select_reduce_fusion
  76.7 229.1 %all-to-all-done.2 = bf16[16,4,256,512]{2,3,1,0:T(8,128)(2,1)} async-done(((bf16[16,4,256,512]{2,3,1,0:T(8,128)(2,1)}), bf16[16,4,256,512]{2,3,1,0:T(8,128)(2,1)}, u32[]{:S(2)}, u32[]{:S(2)}) %all-to-all-start.2) | async-done | bytes 16777248 | tf_op jit(solution)/shard_map/all_to_all | solution.py:28
  305.8 24.3 %copy.33 = bf16[8,8,256,512]{3,1,2,0:T(8,128)(2,1)} copy(bf16[8,8,256,512]{2,3,1,0:T(8,128)(2,1)} %bitcast.36) | data formatting | bytes 33554432
  330.1 9.2 %divide_convert_fusion = bf16[16,256,512]{2,0,1:T(8,128)(2,1)S(1)} fusion(bf16[16,256,512]{2,1,0:T(8,128)(2,1)} %bitcast.54, f32[16]{0:T(128)S(1)} %broadcast_add_fusion, f32[64]{0:T(128)S(1)} %reshape.48, f32[64]{0:T(128)S(1)} %reshape.47, bf16[8,8,256,512]{3,1,2,0:T(8,128)(2,1)} %copy.33), kind=kOutput, calls=%fused_computation.10 | convolution fusion | flops 278923264 | bytes 25166400 | tf_op jit(solution)/shard_map/dot_general | solution.py:42
  339.3 2.4 copy.30
  341.7 0.0 copy-start.4
  341.7 0.0 copy-done
  341.7 5.7 %multiply_convert_fusion.1 = (bf16[4096,512]{1,0:T(8,128)(2,1)S(1)}, f32[4096,512]{1,0:T(8,128)}) fusion(bf16[4096,512]{1,0:T(8,128)(2,1)S(1)} %bitcast.55, bf16[512,512]{1,0:T(8,128)(2,1)S(1)} %copy-done), kind=kOutput, calls=%fused_computation.8 | convolution fusion | flops 2157969408 | bytes 17301504 | tf_op jit(solution)/shard_map/dot_general | solution.py:50
  347.4 0.0 copy-done.4
  347.4 0.0 copy-start.2
  347.4 10.1 %fusion.3 = bf16[512,4096]{0,1:T(8,128)(2,1)S(1)} fusion(bf16[4096,512]{1,0:T(8,128)(2,1)S(1)} %get-tuple-element.15, bf16[512,512]{1,0:T(8,128)(2,1)S(1)} %all_gather.3, s32[512]{0:T(512)S(1)} %bitcast.63, s32[512]{0:T(512)S(1)} %bitcast.64, s32[512]{0:T(512)S(1)} %bitcast.58, s32[512]{0:T(512)S(1)} %bitcast.59, s32[512]{0:T(512)S(1)} %bitcast.60, ...), kind=kOutput, calls=%fused_computation.6 | convolution fusion | flops 2195718144 | bytes 8945664 | tf_op jit(solution)/shard_map/nd,ld->nl/dot_general | solution.py:55
  357.5 0.0 copy-done.2
  357.5 0.0 copy-start.3
  357.5 1.9 copy-done.3
  359.4 3.3 fusion.15
  362.7 0.0 reduce-scatter.2.cloned.1.call-update
  362.7 0.3 all-reduce.6.cloned.1.call-start
  363.0 0.0 copy-start.1
  363.0 12.6 %fusion.6 = f32[512,512]{1,0:T(8,128)} fusion(bf16[4096,512]{1,0:T(8,128)(2,1)} %bitcast.56, f32[4096,512]{1,0:T(8,128)} %get-tuple-element.14, bf16[512,4096]{0,1:T(8,128)(2,1)} %copy-done.3, bf16[512,512]{1,0:T(8,128)(2,1)S(1)} %all_gather.3), kind=kOutput, calls=%fused_computation.11 | convolution fusion | flops 4313841664 | bytes 18350080 | tf_op jit(solution)/shard_map/la,lb->ab/dot_general | solution.py:69
  375.7 21.5 %reduce-scatter.2.cloned.1.call-done = f32[64,512]{1,0:T(8,128)} async-done(((f32[512,512]{1,0:T(8,128)}), f32[64,512]{1,0:T(8,128)}) %reduce-scatter.2.cloned.1.call-update) | async-done | bytes 131088 | tf_op jit(solution)/shard_map/reduce_scatter | solution.py:71
  397.1 0.0 all-reduce.6.cloned.1.call-update
  397.2 0.0 all-reduce.4.cloned.1.call-start
  397.2 89.0 %all-reduce.6.cloned.1.call-done = (f32[64,512]{1,0:T(8,128)}, f32[512,512]{1,0:T(8,128)}) async-done(((f32[64,512]{1,0:T(8,128)}, f32[512,512]{1,0:T(8,128)}), (f32[64,512]{1,0:T(8,128)}, f32[512,512]{1,0:T(8,128)})) %all-reduce.6.cloned.1.call-update) | async-done | bytes 1179664 | tf_op jit(solution)/shard_map/psum | solution.py:72
  486.2 0.0 all-reduce.4.cloned.1.call-update
  486.3 64.4 %all-reduce.4.cloned.1.call-done = f32[512,512]{1,0:T(8,128)} async-done(((f32[512,512]{1,0:T(8,128)}), f32[512,512]{1,0:T(8,128)}) %all-reduce.4.cloned.1.call-update) | async-done | bytes 1048592 | tf_op jit(solution)/shard_map/psum | solution.py:9
  550.7 1.6 copy.45
  552.3 2.3 copy.46
  554.5 0.0 copy-done.1
  (6 shorter events, 0.1 us)
Async XLA Ops:
  7.2 334.5 %copy-start = (bf16[512,512]{1,0:T(8,128)(2,1)S(1)}, bf16[512,512]{1,0:T(8,128)(2,1)}, u32[]{:S(2)}) copy-start(bf16[512,512]{1,0:T(8,128)(2,1)} %param.13) | copy-start | bytes 1572868
  8.6 19.2 %all-to-all-start = ((bf16[16,1,4]{2,1,0:T(2,128)(2,1)}), bf16[16,1,4]{2,1,0:T(2,128)(2,1)S(1)}, u32[]{:S(2)}, u32[]{:S(2)}) async-start(bf16[16,1,4]{2,1,0:T(2,128)(2,1)} %copy.23), calls=%async_computation | async-start | bytes 16384 | tf_op jit(solution)/shard_map/all_to_all | solution.py:29
  27.8 26.5 %all-to-all-start.1 = ((bf16[16,1,4]{2,1,0:T(2,128)(2,1)}), bf16[16,1,4]{2,1,0:T(2,128)(2,1)S(1)}, u32[]{:S(2)}, u32[]{:S(2)}) async-start(bf16[16,1,4]{2,1,0:T(2,128)(2,1)} %copy.24), calls=%async_computation.1 | async-start | bytes 16384 | tf_op jit(solution)/shard_map/all_to_all | solution.py:32
  54.3 7.5 %copy-start.6 = (s32[512,8]{0,1:T(8,128)S(1)}, s32[512,8]{0,1:T(8,128)}, u32[]{:S(2)}) copy-start(s32[512,8]{0,1:T(8,128)} %param.15) | copy-start | bytes 49156
  54.3 7.5 %copy-start.5 = (bf16[64,512]{1,0:T(8,128)(2,1)S(1)}, bf16[64,512]{1,0:T(8,128)(2,1)}, u32[]{:S(2)}) copy-start(bf16[64,512]{1,0:T(8,128)(2,1)} %param.14) | copy-start | bytes 196612
  54.3 251.5 %all-to-all-start.2 = ((bf16[16,4,256,512]{2,3,1,0:T(8,128)(2,1)}), bf16[16,4,256,512]{2,3,1,0:T(8,128)(2,1)}, u32[]{:S(2)}, u32[]{:S(2)}) async-start(bf16[16,4,256,512]{2,3,1,0:T(8,128)(2,1)} %convert_bitcast_fusion), calls=%async_computation.2 | async-start | bytes 33554432 | tf_op jit(solution)/shard_map/all_to_all | solution.py:28
  61.7 335.4 %reduce-scatter.2.cloned.1.call-start = ((), (), s32[]{:S(2)}) async-start(), calls=%async_computation.4 | async-start | bytes 1179648 | tf_op jit(solution)/shard_map/reduce_scatter | solution.py:71
  341.7 5.7 %copy-start.4 = (bf16[16,256,512]{2,1,0:T(8,128)(2,1)}, bf16[16,256,512]{2,1,0:T(8,128)(2,1)S(1)}, u32[]{:S(2)}) copy-start(bf16[16,256,512]{2,1,0:T(8,128)(2,1)S(1)} %copy.30) | copy-start | bytes 12582916
  347.4 10.1 %copy-start.2 = (bf16[4096,512]{1,0:T(8,128)(2,1)}, bf16[4096,512]{1,0:T(8,128)(2,1)S(1)}, u32[]{:S(2)}) copy-start(bf16[4096,512]{1,0:T(8,128)(2,1)S(1)} %get-tuple-element.15) | copy-start | bytes 12582916
  357.5 1.9 copy-start.3
  362.7 123.5 %all-reduce.6.cloned.1.call-start = ((), (), s32[]{:S(2)}) async-start(), calls=%async_computation.6 | async-start | bytes 2359296 | tf_op jit(solution)/shard_map/psum | solution.py:72
  363.0 191.5 %copy-start.1 = (bf16[512,512]{1,0:T(8,128)(2,1)S(1)}, bf16[512,512]{1,0:T(8,128)(2,1)}, u32[]{:S(2)}) copy-start(bf16[512,512]{1,0:T(8,128)(2,1)} %param.13) | copy-start | bytes 1572868
  397.2 153.5 %all-reduce.4.cloned.1.call-start = ((), (), s32[]{:S(2)}) async-start(), calls=%async_computation.5 | async-start | bytes 2097152 | tf_op jit(solution)/shard_map/psum | solution.py:9
Sparse Core Ops, SparseCore 0:
  362.9 34.2 reduce-scatter.1
  400.5 85.6 all-reduce.5
  488.6 62.0 all-reduce.3
